TPU v7x, 32 devices: a whole 2x2x4 slice. The times are simulated.
32 devices in a mesh: bucket: 4 (over y, core), seq: 8 (over z, x).
Axes of the slice: x: 2, y: 2, z: 4, core: 2. Of those that a mesh axis runs over, the one named last changes fastest.
Arguments:
- tokens: bfloat16 [4, 2, 2048, 768], P('bucket', None, 'seq'), may hold values from -6 to 6
- cotangent: bfloat16 [4, 2, 2048, 768], P('bucket', None, 'seq'), may hold values from -6 to 6
- lengths: int32 [4, 2], P('bucket'), may hold values from 128 to 2048, as said below
- decay_rate: float32 [768], replicated, may hold values from 1 to 100
- norm1_gain: bfloat16 [768], replicated, may hold values from 0.5 to 1.5
- norm1_bias: bfloat16 [768], replicated, may hold values from -1.25 to 1.25
- w_in: bfloat16 [768, 2304], replicated, may hold values from -0.21875 to 0.21875
- b_in: bfloat16 [2304], replicated, may hold values from -1.25 to 1.25
- short_weight: bfloat16 [3, 2304], replicated, may hold values from -3 to 3
- short_bias: bfloat16 [2304], replicated, may hold values from -1.25 to 1.25
- filter_w1: bfloat16 [33, 64], replicated, may hold values from -16 to 16
- filter_b1: bfloat16 [64], replicated, may hold values from -3.140625 to 3.140625
- filter_w2: bfloat16 [64, 64], replicated, may hold values from -6 to 6
- filter_b2: bfloat16 [64], replicated, may hold values from -3.140625 to 3.140625
- filter_w3: bfloat16 [64, 768], replicated, may hold values from -0.0625 to 0.0625
- skip_gain: bfloat16 [768], replicated, may hold values from -6 to 6
- w_out: bfloat16 [768, 768], replicated, may hold values from -0.21875 to 0.21875
- b_out: bfloat16 [768], replicated, may hold values from -1.25 to 1.25
- norm2_gain: bfloat16 [768], replicated, may hold values from 0.5 to 1.5
- norm2_bias: bfloat16 [768], replicated, may hold values from -1.25 to 1.25
- mlp_w1: bfloat16 [768, 3072], replicated, may hold values from -0.21875 to 0.21875
- mlp_b1: bfloat16 [3072], replicated, may hold values from -1.25 to 1.25
- mlp_w2: bfloat16 [3072, 768], replicated, may hold values from -0.109375 to 0.109375
- mlp_b2: bfloat16 [768], replicated, may hold values from -1.25 to 1.25
Outputs:
- output: bfloat16 [4, 2, 2048, 768], P('bucket', None, 'seq')
- tokens_grad: float32 [4, 2, 2048, 768], P('bucket', None, 'seq')
- grad_norm1_gain: float32 [768], replicated
- grad_norm1_bias: float32 [768], replicated
- grad_w_in: float32 [768, 2304], replicated
- grad_b_in: float32 [2304], replicated
- grad_short_weight: float32 [3, 2304], replicated
- grad_short_bias: float32 [2304], replicated
- grad_filter_w1: float32 [33, 64], replicated
- grad_filter_b1: float32 [64], replicated
- grad_filter_w2: float32 [64, 64], replicated
- grad_filter_b2: float32 [64], replicated
- grad_filter_w3: float32 [64, 768], replicated
- grad_skip_gain: float32 [768], replicated
- grad_w_out: float32 [768, 768], replicated
- grad_b_out: float32 [768], replicated
- grad_norm2_gain: float32 [768], replicated
- grad_norm2_bias: float32 [768], replicated
- grad_mlp_w1: float32 [768, 3072], replicated
- grad_mlp_b1: float32 [3072], replicated
- grad_mlp_w2: float32 [3072, 768], replicated
- grad_mlp_b2: float32 [768], replicated
Inputs may be any that keep to these rules, and one draw needn't show every extreme that they name: `lengths`: every value lies between 128 and 2048, and some sequence has length exactly 2048.
All inputs are finite; a program needn't handle non-finite values.
Results may differ from a plain program's by a relative error of at most 0.012.
Values may be sent and summed in bfloat16 or wider, within the bound.
No kernel may reach another device: no remote copies, remote signals or barrier semaphores. Data moves between devices by JAX's collectives and lax.ppermute only.
A program may use at most 320 MiB of HBM per device.

v0:
```python
import math

import jax
import jax.numpy as jnp
from jax import lax
from jax.sharding import PartitionSpec as P

HIGH = lax.Precision.HIGHEST
SPECTRAL = lax.Precision.HIGH
EPSILON = 1e-05


def passed_along(block, axis, distance):
    devices = range(lax.axis_size(axis))
    route = [(i - distance, i) for i in devices if i - distance in devices]
    return lax.ppermute(block, axis, route)


def rounded(values):
    return lax.optimization_barrier(values.astype(jnp.bfloat16)).astype(jnp.float32)


def precise(formula, left, right):
    return jnp.einsum(formula, left, right, precision=HIGH, preferred_element_type=jnp.float32)


def spectral(formula, left, right):
    return jnp.einsum(formula, left, right, precision=SPECTRAL, preferred_element_type=jnp.float32)


def lowmul(formula, left, right):
    return jnp.einsum(formula, left, right, preferred_element_type=jnp.float32)


def position_features(length):
    steps = jnp.arange(length, dtype=jnp.int32).astype(jnp.float32)
    bands = 0.0001 + jnp.arange(16, dtype=jnp.int32).astype(jnp.float32) * ((15.0 - 0.0001) / 15.0)
    phase = 2.0 * math.pi / length * steps[:, None] * bands[None, :]
    return jnp.concatenate([(steps / length)[:, None], jnp.cos(phase), -jnp.sin(phase)], axis=1)


def filter_values(filter_w1, filter_b1, filter_w2, filter_b2, filter_w3, rates, length):
    feats = position_features(length)
    hidden = jnp.sin(precise("pe,eh->ph", feats, filter_w1) + filter_b1)
    hidden = jnp.sin(precise("ph,hk->pk", hidden, filter_w2) + filter_b2)
    shaped = precise("ph,hd->pd", hidden, filter_w3)
    times = jnp.arange(length, dtype=jnp.int32).astype(jnp.float32)[:, None] / length
    return shaped * (jnp.exp(-times * rates[None, :]) + 0.05)


def norm_forward(values, gain, bias):
    center = values - jnp.mean(values, axis=-1, keepdims=True)
    inverse = lax.rsqrt(jnp.mean(center * center, axis=-1, keepdims=True) + EPSILON)
    unit = center * inverse
    return (unit * gain + bias, unit, inverse)


def norm_backward(grad_out, gain, unit, inverse):
    scaled = grad_out * gain
    grad_in = inverse * (
        scaled
        - jnp.mean(scaled, axis=-1, keepdims=True)
        - unit * jnp.mean(scaled * unit, axis=-1, keepdims=True)
    )
    return (grad_in, jnp.sum(grad_out * unit, axis=0), jnp.sum(grad_out, axis=0))


def transform_tables(block_len):
    freqs = jnp.arange(block_len, dtype=jnp.int32)[:, None]
    spots = jnp.arange(2 * block_len, dtype=jnp.int32)[None, :]
    angle = math.pi / block_len * (freqs * spots % (2 * block_len)).astype(jnp.float32)
    sign_row = (1 - 2 * (spots % 2)).astype(jnp.float32)
    fwd_real = jnp.cos(angle)
    fwd_imag = jnp.where(freqs == 0, sign_row, -jnp.sin(angle))
    later = spots[:, block_len:]
    inv_angle = math.pi / block_len * (freqs * later % (2 * block_len)).astype(jnp.float32)
    scale = 1.0 / (2 * block_len)
    inv_real = jnp.where(freqs == 0, scale, 2.0 * scale * jnp.cos(inv_angle)).T
    inv_imag = jnp.where(
        freqs == 0, scale * sign_row[:, block_len:], -2.0 * scale * jnp.sin(inv_angle)
    ).T
    upper = (freqs >= 1).astype(jnp.float32)
    return (fwd_real, fwd_imag, inv_real, inv_imag, upper)


def combine_forward(first_real, first_imag, second_real, second_imag, upper):
    real = first_real * second_real - upper * first_imag * second_imag
    imag = (
        upper * (first_real * second_imag + first_imag * second_real)
        + (1.0 - upper) * first_imag * second_imag
    )
    return (real, imag)


def combine_back(fixed_real, fixed_imag, grad_real, grad_imag, upper):
    real = fixed_real * grad_real + upper * fixed_imag * grad_imag
    imag = (
        upper * (fixed_real * grad_imag - fixed_imag * grad_real)
        + (1.0 - upper) * fixed_imag * grad_imag
    )
    return (real, imag)


def local(
    tokens,
    cotangent,
    lengths,
    decay_rate,
    norm1_gain,
    norm1_bias,
    w_in,
    b_in,
    short_weight,
    short_bias,
    filter_w1,
    filter_b1,
    filter_w2,
    filter_b2,
    filter_w3,
    skip_gain,
    w_out,
    b_out,
    norm2_gain,
    norm2_bias,
    mlp_w1,
    mlp_b1,
    mlp_w2,
    mlp_b2,
):
    seq_count = tokens.shape[1]
    block_len = tokens.shape[2]
    model_width = tokens.shape[3]
    row_count = seq_count * block_len
    block_count = lax.axis_size("seq")
    full_len = block_count * block_len
    position = lax.axis_index("seq")
    places = position * block_len + jnp.arange(block_len, dtype=jnp.int32)
    valid = (places[None, :] < lengths[0][:, None]).astype(jnp.float32).reshape(row_count, 1)
    inputs = tokens.reshape(row_count, model_width).astype(jnp.float32)
    gain_one = norm1_gain.astype(jnp.float32)
    gain_two = norm2_gain.astype(jnp.float32)
    taps = short_weight.astype(jnp.float32)
    skip = skip_gain.astype(jnp.float32)
    normed, unit_one, inverse_one = norm_forward(inputs, gain_one, norm1_bias.astype(jnp.float32))
    normed_low = normed.astype(jnp.bfloat16)
    mixed = jnp.dot(normed_low, w_in, preferred_element_type=jnp.float32) + b_in.astype(jnp.float32)
    mixed_low = mixed.astype(jnp.bfloat16).reshape(seq_count, block_len, 3 * model_width)
    edge = passed_along(mixed_low[:, block_len - 2 :, :], "seq", 1)
    extended = jnp.concatenate([edge, mixed_low], axis=1).astype(jnp.float32)
    conv = (
        taps[0] * extended[:, 2:]
        + taps[1] * extended[:, 1:-1]
        + taps[2] * extended[:, :-2]
        + short_bias.astype(jnp.float32)
    )
    gate_out = conv[:, :, :model_width]
    gate_in = conv[:, :, model_width : 2 * model_width]
    values = conv[:, :, 2 * model_width :]
    signal_low = (values * gate_in).astype(jnp.bfloat16)
    signal = signal_low.astype(jnp.float32)

    def filter_fn(weight_one, bias_first, weight_two, bias_second, weight_three):
        return filter_values(
            weight_one, bias_first, weight_two, bias_second, weight_three, decay_rate, full_len
        )

    raw_filter, filter_pull = jax.vjp(
        filter_fn,
        filter_w1.astype(jnp.float32),
        filter_b1.astype(jnp.float32),
        filter_w2.astype(jnp.float32),
        filter_b2.astype(jnp.float32),
        filter_w3.astype(jnp.float32),
    )
    filt = rounded(raw_filter)
    fwd_real, fwd_imag, inv_real, inv_imag, upper = transform_tables(block_len)
    head_real = fwd_real[:, :block_len]
    head_imag = fwd_imag[:, :block_len]
    tail_real = fwd_real[:, block_len:]
    tail_imag = fwd_imag[:, block_len:]
    padded = jnp.concatenate(
        [jnp.zeros((block_len, model_width), jnp.float32), filt], axis=0
    ).reshape(block_count + 1, block_len, model_width)
    spec_real = spectral("fp,kpd->kfd", head_real, padded[:-1]) + spectral(
        "fp,kpd->kfd", tail_real, padded[1:]
    )
    spec_imag = spectral("fp,kpd->kfd", head_imag, padded[:-1]) + spectral(
        "fp,kpd->kfd", tail_imag, padded[1:]
    )
    sig_real = spectral("fp,spd->sfd", head_real, signal)
    sig_imag = spectral("fp,spd->sfd", head_imag, signal)

    def add_earlier(totals, source, source_real, source_imag):
        lag = position - source
        weight = (lag >= 0).astype(jnp.float32)
        lag_safe = jnp.maximum(lag, 0)
        filt_real = lax.dynamic_index_in_dim(spec_real, lag_safe, 0, keepdims=False)
        filt_imag = lax.dynamic_index_in_dim(spec_imag, lag_safe, 0, keepdims=False)
        part_real, part_imag = combine_forward(
            filt_real, filt_imag, source_real, source_imag, upper
        )
        return (totals[0] + weight * part_real, totals[1] + weight * part_imag)

    empty = jnp.zeros((seq_count, block_len, model_width), jnp.float32)
    piece = (
        lax.all_gather(sig_real[None], "seq", axis=0, tiled=True),
        lax.all_gather(sig_imag[None], "seq", axis=0, tiled=True),
    )

    def one_block(index, inner):
        return add_earlier(
            inner,
            index,
            lax.dynamic_index_in_dim(piece[0], index, 0, keepdims=False),
            lax.dynamic_index_in_dim(piece[1], index, 0, keepdims=False),
        )

    long_real, long_imag = lax.fori_loop(0, piece[0].shape[0], one_block, (empty, empty))
    conv_long = spectral("nf,sfd->snd", inv_real, long_real) + spectral(
        "nf,sfd->snd", inv_imag, long_imag
    )
    long_out = conv_long + signal * skip
    gated_low = (long_out * gate_out).astype(jnp.bfloat16).reshape(row_count, model_width)
    branch = jnp.dot(gated_low, w_out, preferred_element_type=jnp.float32) + b_out.astype(
        jnp.float32
    )
    resid = inputs + branch
    normed_two, unit_two, inverse_two = norm_forward(
        resid, gain_two, norm2_bias.astype(jnp.float32)
    )
    normed_two_low = normed_two.astype(jnp.bfloat16)
    pre = jnp.dot(normed_two_low, mlp_w1, preferred_element_type=jnp.float32) + mlp_b1.astype(
        jnp.float32
    )
    active_low = jax.nn.gelu(pre, approximate=False).astype(jnp.bfloat16)
    final = (
        resid
        + jnp.dot(active_low, mlp_w2, preferred_element_type=jnp.float32)
        + mlp_b2.astype(jnp.float32)
    )
    output = (final * valid).astype(jnp.bfloat16).reshape(1, seq_count, block_len, model_width)
    grad_final_low = (cotangent.reshape(row_count, model_width).astype(jnp.float32) * valid).astype(
        jnp.bfloat16
    )
    grad_final = grad_final_low.astype(jnp.float32)
    grad_mlp_b2 = jnp.sum(grad_final, axis=0)
    grad_mlp_w2 = lowmul("rh,rd->hd", active_low, grad_final_low)
    grad_active = lowmul("rd,hd->rh", grad_final_low, mlp_w2)
    cumulative = 0.5 * (1.0 + lax.erf(pre * (1.0 / math.sqrt(2.0))))
    density = jnp.exp(-0.5 * pre * pre) * (1.0 / math.sqrt(2.0 * math.pi))
    grad_pre_low = (grad_active * (cumulative + pre * density)).astype(jnp.bfloat16)
    grad_mlp_b1 = jnp.sum(grad_pre_low.astype(jnp.float32), axis=0)
    grad_mlp_w1 = lowmul("rd,rh->dh", normed_two_low, grad_pre_low)
    grad_normed_two = lowmul("rh,dh->rd", grad_pre_low, mlp_w1)
    grad_resid_norm, grad_norm2_gain, grad_norm2_bias = norm_backward(
        grad_normed_two, gain_two, unit_two, inverse_two
    )
    grad_resid = grad_final + grad_resid_norm
    grad_branch_low = grad_resid.astype(jnp.bfloat16)
    grad_b_out = jnp.sum(grad_branch_low.astype(jnp.float32), axis=0)
    grad_w_out = lowmul("rd,re->de", gated_low, grad_branch_low)
    grad_gated = lowmul("re,de->rd", grad_branch_low, w_out).reshape(
        seq_count, block_len, model_width
    )
    grad_long_low = (grad_gated * gate_out).astype(jnp.bfloat16)
    grad_long = grad_long_low.astype(jnp.float32)
    grad_gate_out = grad_gated * long_out
    grad_skip_gain = jnp.sum(grad_long * signal, axis=(0, 1))
    back_real = spectral("nf,snd->sfd", inv_real, grad_long)
    back_imag = spectral("nf,snd->sfd", inv_imag, grad_long)

    def add_later(totals, source, source_real, source_imag):
        lag = source - position
        weight = (lag >= 0).astype(jnp.float32)
        lag_safe = jnp.maximum(lag, 0)
        filt_real = lax.dynamic_index_in_dim(spec_real, lag_safe, 0, keepdims=False)
        filt_imag = lax.dynamic_index_in_dim(spec_imag, lag_safe, 0, keepdims=False)
        own_real, own_imag = combine_back(filt_real, filt_imag, source_real, source_imag, upper)
        lag_real, lag_imag = combine_back(sig_real, sig_imag, source_real, source_imag, upper)
        old_real = lax.dynamic_index_in_dim(totals[2], lag_safe, 0, keepdims=False)
        old_imag = lax.dynamic_index_in_dim(totals[3], lag_safe, 0, keepdims=False)
        new_real = lax.dynamic_update_index_in_dim(
            totals[2], old_real + weight * jnp.sum(lag_real, axis=0), lag_safe, 0
        )
        new_imag = lax.dynamic_update_index_in_dim(
            totals[3], old_imag + weight * jnp.sum(lag_imag, axis=0), lag_safe, 0
        )
        return (totals[0] + weight * own_real, totals[1] + weight * own_imag, new_real, new_imag)

    lag_empty = jnp.zeros((block_count, block_len, model_width), jnp.float32)
    absorb_piece = (
        lax.all_gather(back_real[None], "seq", axis=0, tiled=True),
        lax.all_gather(back_imag[None], "seq", axis=0, tiled=True),
    )

    def one_block(index, inner):
        return add_later(
            inner,
            index,
            lax.dynamic_index_in_dim(absorb_piece[0], index, 0, keepdims=False),
            lax.dynamic_index_in_dim(absorb_piece[1], index, 0, keepdims=False),
        )

    own_real, own_imag, lags_real, lags_imag = lax.fori_loop(
        0, absorb_piece[0].shape[0], one_block, (empty, empty, lag_empty, lag_empty)
    )
    grad_signal = (
        grad_long * skip
        + spectral("fp,sfd->spd", head_real, own_real)
        + spectral("fp,sfd->spd", head_imag, own_imag)
    )
    lag_head = spectral("fp,kfd->kpd", head_real, lags_real) + spectral(
        "fp,kfd->kpd", head_imag, lags_imag
    )
    lag_tail = spectral("fp,kfd->kpd", tail_real, lags_real) + spectral(
        "fp,kfd->kpd", tail_imag, lags_imag
    )
    grad_filter = (
        lag_tail
        + jnp.concatenate(
            [lag_head[1:], jnp.zeros((1, block_len, model_width), jnp.float32)], axis=0
        )
    ).reshape(full_len, model_width)
    grad_filter_w1, grad_filter_b1, grad_filter_w2, grad_filter_b2, grad_filter_w3 = filter_pull(
        grad_filter
    )
    grad_conv = jnp.concatenate(
        [grad_gate_out, grad_signal * values, grad_signal * gate_in], axis=2
    )
    grad_short_bias = jnp.sum(grad_conv, axis=(0, 1))
    grad_short_weight = jnp.stack(
        [
            jnp.sum(grad_conv * extended[:, 2:], axis=(0, 1)),
            jnp.sum(grad_conv * extended[:, 1:-1], axis=(0, 1)),
            jnp.sum(grad_conv * extended[:, :-2], axis=(0, 1)),
        ]
    )
    grad_extended = (
        jnp.pad(taps[0] * grad_conv, ((0, 0), (2, 0), (0, 0)))
        + jnp.pad(taps[1] * grad_conv, ((0, 0), (1, 1), (0, 0)))
        + jnp.pad(taps[2] * grad_conv, ((0, 0), (0, 2), (0, 0)))
    )
    returned = passed_along(grad_extended[:, :2], "seq", -1)
    grad_mixed = grad_extended[:, 2:] + jnp.pad(returned, ((0, 0), (block_len - 2, 0), (0, 0)))
    grad_mixed_low = grad_mixed.astype(jnp.bfloat16).reshape(row_count, 3 * model_width)
    grad_b_in = jnp.sum(grad_mixed_low.astype(jnp.float32), axis=0)
    grad_w_in = lowmul("rd,rk->dk", normed_low, grad_mixed_low)
    grad_normed = lowmul("rk,dk->rd", grad_mixed_low, w_in)
    grad_input_norm, grad_norm1_gain, grad_norm1_bias = norm_backward(
        grad_normed, gain_one, unit_one, inverse_one
    )
    tokens_grad = (grad_resid + grad_input_norm).reshape(1, seq_count, block_len, model_width)
    all_sums = lax.psum(
        (
            grad_norm1_gain,
            grad_norm1_bias,
            grad_w_in,
            grad_b_in,
            grad_short_weight,
            grad_short_bias,
            grad_filter_w1,
            grad_filter_b1,
            grad_filter_w2,
            grad_filter_b2,
            grad_filter_w3,
            grad_skip_gain,
            grad_norm2_gain,
            grad_norm2_bias,
            grad_mlp_w1,
            grad_mlp_b1,
            grad_mlp_w2,
            grad_mlp_b2,
            grad_w_out,
            grad_b_out,
        ),
        ("bucket", "seq"),
    )
    summed = tuple(all_sums)
    return (
        output,
        tokens_grad,
        summed[0],
        summed[1],
        summed[2],
        summed[3],
        summed[4],
        summed[5],
        summed[6],
        summed[7],
        summed[8],
        summed[9],
        summed[10],
        summed[11],
        summed[18],
        summed[19],
        summed[12],
        summed[13],
        summed[14],
        summed[15],
        summed[16],
        summed[17],
    )


def solution(mesh):
    in_specs = (
        P("bucket", None, "seq", None),
        P("bucket", None, "seq", None),
        P("bucket", None),
        P(),
        P(),
        P(),
        P(),
        P(),
        P(),
        P(),
        P(),
        P(),
        P(),
        P(),
        P(),
        P(),
        P(),
        P(),
        P(),
        P(),
        P(),
        P(),
        P(),
        P(),
    )
    out_specs = (
        P("bucket", None, "seq", None),
        P("bucket", None, "seq", None),
        P(),
        P(),
        P(),
        P(),
        P(),
        P(),
        P(),
        P(),
        P(),
        P(),
        P(),
        P(),
        P(),
        P(),
        P(),
        P(),
        P(),
        P(),
        P(),
        P(),
    )
    return jax.shard_map(local, mesh=mesh, in_specs=in_specs, out_specs=out_specs, check_vma=False)
```

profile of v0, /device:TPU:0, one launch (start us, length us, event | category | flops | bytes accessed | tf_op | source)
XLA Modules:
  0.0 1675.5 jit_solution(14058098779002749714)
XLA Ops:
  72.8 6.6 copy.110
  79.4 7.7 fusion.92
  92.6 6.6 copy.111
  105.1 107.3 %all-gather.9.cloned.1.call-done = f32[16,256,768]{2,1,0:T(8,128)} async-done(((f32[2,256,768]{2,1,0:T(8,128)}), f32[16,256,768]{2,1,0:T(8,128)}) %all-gather.9.cloned.1.call-update) | async-done | bytes 12582928 | tf_op jit(solution)/shard_map/all_gather | solution.py:206
  212.4 176.8 %all-gather.11.cloned.1.call-done = f32[16,256,768]{2,1,0:T(8,128)} async-done(((f32[2,256,768]{2,1,0:T(8,128)}), f32[16,256,768]{2,1,0:T(8,128)}) %all-gather.11.cloned.1.call-update) | async-done | bytes 12582928 | tf_op jit(solution)/shard_map/all_gather | solution.py:207
  389.2 74.0 %while.38 = (s32[]{:T(128)}, f32[2,256,768]{2,1,0:T(8,128)}, f32[2,256,768]{2,1,0:T(8,128)}, s32[]{:T(128)}, f32[8,256,768]{2,1,0:T(8,128)}, /*index=5*/f32[8,2,...) while((s32[]{:T(128)}, f32[2,256,768]{2,1,0:T(8,128)}, ...), condition=%wide.region_3.4_spmd.clone.clone, body=%wide.region_2.3_spmd.clone.clone.sunk | while | flops 6292231 | bytes 17307816 | solution.py:218
  400.8 6.2 fusion.217
  410.1 6.2 fusion.217
  419.5 6.2 fusion.217
  428.9 6.3 fusion.217
  438.3 6.2 fusion.217
  447.7 6.2 fusion.217
  457.0 6.2 fusion.217
  471.9 19.9 %fusion.30 = (bf16[512,3072]{1,0:T(8,128)(2,1)}, f32[512,3072]{1,0:T(8,128)S(1)}) fusion(f32[3072]{0:T(1024)S(1)} %copy-done.86, bf16[768,3072]{1,0:T(8,128)(2,1)} %param.48, f32[512,768]{1,0:T(8,128)S(1)} %get-tuple-element.727, f32[768]{0:T(1024)S(1)} %copy-done.98, f32[768]{0:T(1024)S(1)} %copy-done.81, f32[512]{0:T(512)S(1)} %add_rsqrt_fusion, ...), kind=kOutput, calls=%fused_computation.60 | convolution fusion | flops 2521694208 | bytes 15751168 | tf_op jit(solution)/shard_map/dot_general | solution.py:232
  539.5 148.3 %all-gather.13.cloned.1.call-done = f32[16,256,768]{2,1,0:T(8,128)} async-done(((f32[2,256,768]{2,1,0:T(8,128)}), f32[16,256,768]{2,1,0:T(8,128)}) %all-gather.13.cloned.1.call-update) | async-done | bytes 12582928 | tf_op jit(solution)/shard_map/all_gather | solution.py:292
  687.8 176.7 %all-gather.15.cloned.1.call-done = f32[16,256,768]{2,1,0:T(8,128)} async-done(((f32[2,256,768]{2,1,0:T(8,128)}), f32[16,256,768]{2,1,0:T(8,128)}) %all-gather.15.cloned.1.call-update) | async-done | bytes 12582928 | tf_op jit(solution)/shard_map/all_gather | solution.py:293
  870.9 113.2 %while.39 = (s32[]{:T(128)}, f32[2,256,768]{2,1,0:T(8,128)}, f32[2,256,768]{2,1,0:T(8,128)}, f32[8,256,768]{2,1,0:T(8,128)}, f32[8,256,768]{2,1,0:T(8,128)}, /*i...) while((s32[]{:T(128)}, f32[2,256,768]{2,1,0:T(8,128)}, ...), condition=%wide.region_11.12_spmd.clone.clone, body=%wide.region_8.11_spmd.clone.clone.sunk | while | flops 11797255 | bytes 26746068 | solution.py:304
  888.9 6.8 fusion.218
  903.2 6.8 fusion.218
  917.4 6.8 fusion.218
  931.7 6.8 fusion.218
  946.0 6.8 fusion.218
  960.2 6.8 fusion.218
  974.5 6.8 fusion.218
  991.5 6.7 multiply_reduce_fusion.2
  999.3 7.2 pad_add_fusion
  1053.3 6.9 fusion.160
  1060.9 7.4 multiply_convert_fusion.3
  1070.0 118.8 %all-reduce.11.cloned.1.call-done = (f32[768]{0:T(1024)}, f32[768]{0:T(1024)}, f32[2304]{0:T(1024)}, f32[3,2304]{1,0:T(4,128)}, f32[2304]{0:T(1024)}, /*index=5*...) async-done(((f32[768]{0:T(1024)}, f32[768]{0:T(1024)}, ...) | async-done | bytes 105232 | tf_op jit(solution)/shard_map/psum | solution.py:353
  1188.8 447.9 %all-reduce.13.cloned.1.call-done = (f32[768,2304]{1,0:T(8,128)}, f32[64,768]{1,0:T(8,128)}, f32[768,768]{1,0:T(8,128)}, f32[768,3072]{1,0:T(8,128)}, f32[3072,768]{1,0:T(8,128)}) async-done(((f32[768,2304]{1,0:T(8,128)}, f32[64,768]{1,0:T(8,128)}, f32[768,768]{1,0:T(8,128)}, f32[768,3072]{1,0:T(8,128)}, f32[3072,768]{1,0:T(8,128)}), (f32[768,2304]{1,0:T(8,128)}, f32[64,768]{1,0:T(8,128)}, ...) | async-done | bytes 28508176 | tf_op jit(solution)/shard_map/psum | solution.py:353
  1639.4 6.6 copy.205
  1654.5 8.8 copy.219
  (476 shorter events, 308.2 us)
Async XLA Ops:
  7.2 205.2 %all-gather.9.cloned.1.call-start = ((), (), s32[]{:S(2)}) async-start(), calls=%async_computation | async-start | bytes 14155776 | tf_op jit(solution)/shard_map/all_gather | solution.py:206
  16.7 6.9 collective-permute-start
  34.4 354.8 %all-gather.11.cloned.1.call-start = ((), (), s32[]{:S(2)}) async-start(), calls=%async_computation.1 | async-start | bytes 14155776 | tf_op jit(solution)/shard_map/all_gather | solution.py:207
  40.9 11.8 copy-start.56
  44.0 643.8 %all-gather.13.cloned.1.call-start = ((), (), s32[]{:S(2)}) async-start(), calls=%async_computation.2 | async-start | bytes 14155776 | tf_op jit(solution)/shard_map/all_gather | solution.py:292
  46.9 9.5 copy-start.52
  46.9 9.5 copy-start.96
  102.3 398.4 %copy-start.68 = (f32[1,2,2,128]{3,1,2,0:T(2,128)}, f32[1,2,2,128]{3,1,2,0:T(2,128)S(1)}, u32[]{:S(2)}) copy-start(f32[1,2,2,128]{3,1,2,0:T(2,128)S(1)} %copy.156) | copy-start | bytes 6148
  102.3 364.4 %copy-start.79 = (s32[1,256]{1,0:T(1,128)}, s32[1,256]{1,0:T(1,128)S(1)}, u32[]{:S(2)}) copy-start(s32[1,256]{1,0:T(1,128)S(1)} %iota_add_fusion) | copy-start | bytes 3076
  470.5 21.2 %slice-start.15 = ((s8[4718592]{0:T(1024)(128)(4,1)}), s8[4194304]{0:T(1024)(128)(4,1)S(1)}, s32[]{:S(2)}) async-start(s8[4718592]{0:T(1024)(128)(4,1)} %bitcast.352), calls=%async_computation.21 | async-start | bytes 8388608
  470.5 26.5 %slice-start.13 = ((s8[4718592]{0:T(1024)(128)(4,1)}), s8[4194304]{0:T(1024)(128)(4,1)S(1)}, s32[]{:S(2)}) async-start(s8[4718592]{0:T(1024)(128)(4,1)} %bitcast.350), calls=%async_computation.19 | async-start | bytes 8388608
  471.4 29.2 %copy-start.27 = (f32[512,768]{1,0:T(8,128)}, f32[512,768]{1,0:T(8,128)S(1)}, u32[]{:S(2)}) copy-start(f32[512,768]{1,0:T(8,128)S(1)} %get-tuple-element.727) | copy-start | bytes 4718596
  471.5 29.2 %copy-start.70 = (f32[512]{0:T(512)}, f32[512]{0:T(512)S(1)}, u32[]{:S(2)}) copy-start(f32[512]{0:T(512)S(1)} %broadcast_multiply_fusion.7) | copy-start | bytes 6148
  471.8 28.9 %copy-start.92 = (f32[512]{0:T(512)}, f32[512]{0:T(512)S(1)}, u32[]{:S(2)}) copy-start(f32[512]{0:T(512)S(1)} %add_rsqrt_fusion) | copy-start | bytes 6148
  471.8 19.9 %copy-start.43 = (bf16[512,768]{1,0:T(8,128)(2,1)S(1)}, bf16[512,768]{1,0:T(8,128)(2,1)}, u32[]{:S(2)}) copy-start(bf16[512,768]{1,0:T(8,128)(2,1)} %fusion.50) | copy-start | bytes 2359300
  471.8 19.9 %slice-start.16 = ((s8[4718592]{0:T(1024)(128)(4,1)}), s8[524288]{0:T(1024)(128)(4,1)S(1)}, s32[]{:S(2)}) async-start(s8[4718592]{0:T(1024)(128)(4,1)} %bitcast.352), calls=%async_computation.22 | async-start | bytes 1048576
  471.9 25.2 %slice-start.14 = ((s8[4718592]{0:T(1024)(128)(4,1)}), s8[524288]{0:T(1024)(128)(4,1)S(1)}, s32[]{:S(2)}) async-start(s8[4718592]{0:T(1024)(128)(4,1)} %bitcast.350), calls=%async_computation.20 | async-start | bytes 1048576
  513.0 351.5 %all-gather.15.cloned.1.call-start = ((), (), s32[]{:S(2)}) async-start(), calls=%async_computation.3 | async-start | bytes 14155776 | tf_op jit(solution)/shard_map/all_gather | solution.py:293
  520.3 668.5 %all-reduce.11.cloned.1.call-start = ((), (), s32[]{:S(2)}) async-start(), calls=%async_computation.4 | async-start | bytes 313344 | tf_op jit(solution)/shard_map/psum | solution.py:353
  1014.6 33.2 %collective-permute-start.1 = (f32[2,2,2304]{2,1,0:T(2,128)S(1)}, f32[2,2,2304]{2,1,0:T(2,128)S(1)}, u32[]{:S(2)}, u32[]{:S(2)}) collective-permute-start(f32[2,2,2304]{2,1,0:T(2,128)S(1)} %pad_add_fusion.1), channel_id=1, source_target_pairs={{1,0},{2,1},{3,2},{4,3},{5,4},{6,5},{7,6},{9,8},{10,9},{11,10},{12... | collective-permute-start | bytes 110600 | tf_op jit(solution)/shard_map/ppermute | solution.py:16
  1036.1 11.7 slice-start.8
  1036.2 10.5 copy-start.39
  1036.2 10.5 copy-start.41
  1036.2 10.5 copy-start.55
  1036.2 11.6 slice-start.9
  1053.2 583.5 %all-reduce.13.cloned.1.call-start = ((), (), s32[]{:S(2)}) async-start(), calls=%async_computation.5 | async-start | bytes 57016320 | tf_op jit(solution)/shard_map/psum | solution.py:353
  1639.3 9.6 copy-start.66
  1639.3 10.2 copy-start.110
  1639.3 10.7 copy-start.45
  1639.3 11.4 copy-start.105
  1639.4 12.0 copy-start.32
  1651.3 12.6 slice-start.10
  (108 other events, 518.2 us)
Sparse Core Ops, SparseCore 0:
  34.5 177.8 all-gather.8
  214.6 174.6 all-gather.10
  513.1 174.5 all-gather.12
  689.8 174.6 all-gather.14
  1053.3 135.4 all-reduce.10
  1196.8 439.8 all-reduce.12
where the time goes:
time: 1690 us; the launch traced here: 1680 us
  waiting for transfers between devices  1180 us (70%)
  other arithmetic  224 us (13%)
  matrix products  160 us (9%)
  local copies, waits for them, and re-layouts  92.6 us (5%)
    psum x2, waiting for transfers between devices, local(): lax.psum((grad_norm1_gain, grad_norm1_bias, grad_w_in, grad_b_in, grad_sh...  567 us
    all_gather x1, waiting for transfers between devices, local(): lax.all_gather(sig_imag[None], 'seq', axis=0, tiled=True)  177 us
    all_gather x1, waiting for transfers between devices, local(): lax.all_gather(back_imag[None], 'seq', axis=0, tiled=True)  177 us
    all_gather x1, waiting for transfers between devices, local(): lax.all_gather(back_real[None], 'seq', axis=0, tiled=True)  148 us
    all_gather x1, waiting for transfers between devices, local(): lax.all_gather(sig_real[None], 'seq', axis=0, tiled=True)  107 us
    dot_general x16, matrix products, spectral(): jnp.einsum(formula, left, right, precision=SPECTRAL, preferred_element_ty...  69 us
    unnamed x289, local copies, waits for them, and re-layouts  53.7 us
    reduce_sum x8, other arithmetic, add_later(): jnp.sum(lag_imag, axis=0)  53.6 us
  transfers between devices with their start and end apart: 8, of which 6 were waited for; matrix products, arithmetic and copies ran while one was open for 9% of the time, Pallas kernels for 0%

commit v1 on v0

v1 whole, which is shorter than its diff:
```python
import math

import jax
import jax.numpy as jnp
import numpy as np
from jax import lax
from jax.experimental import pallas as pl
from jax.experimental.pallas import tpu as pltpu
from jax.sharding import PartitionSpec as P

HIGH = lax.Precision.HIGHEST
EPSILON = 1e-05
F32 = jnp.float32
BF16 = jnp.bfloat16


def norm_forward(values, gain, bias):
    center = values - jnp.mean(values, axis=-1, keepdims=True)
    inverse = lax.rsqrt(jnp.mean(center * center, axis=-1, keepdims=True) + EPSILON)
    unit = center * inverse
    return (unit * gain + bias, unit, inverse)


def norm_backward(grad_out, gain, unit, inverse):
    scaled = grad_out * gain
    grad_in = inverse * (
        scaled
        - jnp.mean(scaled, axis=-1, keepdims=True)
        - unit * jnp.mean(scaled * unit, axis=-1, keepdims=True)
    )
    return (grad_in, jnp.sum(grad_out * unit, axis=0), jnp.sum(grad_out, axis=0))


def precise(formula, left, right):
    return jnp.einsum(formula, left, right, precision=HIGH, preferred_element_type=F32)


def dot(left, right, dims):
    return lax.dot_general(left, right, (dims, ((), ())), preferred_element_type=F32)


def position_features(length):
    steps = lax.broadcasted_iota(jnp.int32, (1, length), 1).astype(F32)
    bands = 0.0001 + lax.broadcasted_iota(jnp.int32, (16, 1), 0).astype(F32) * (
        (15.0 - 0.0001) / 15.0
    )
    phase = 2.0 * math.pi / length * steps * bands
    return jnp.concatenate([steps / length, jnp.cos(phase), -jnp.sin(phase)], axis=0)


def filter_values(weight_one, bias_one, weight_two, bias_two, weight_three, rates, length):
    feats = position_features(length)
    hidden = jnp.sin(precise("eh,ep->hp", weight_one, feats) + bias_one[:, None])
    hidden = jnp.sin(precise("hk,hp->kp", weight_two, hidden) + bias_two[:, None])
    shaped = precise("hd,hp->dp", weight_three, hidden)
    times = lax.broadcasted_iota(jnp.int32, (1, length), 1).astype(F32) / length
    return shaped * (jnp.exp(-times * rates[:, None]) + 0.05)


def transform_tables(block):
    spots = np.arange(block, dtype=np.float64)
    angle = np.pi / block * (spots[None, :] + 0.5) * spots[:, None]
    table = np.concatenate([np.cos(angle), -np.sin(angle)], axis=1)
    high = table.astype(np.float32).astype(jnp.bfloat16)
    low = (table - high.astype(np.float64)).astype(np.float32).astype(jnp.bfloat16)
    back = (table / block).T
    back_high = back.astype(np.float32).astype(jnp.bfloat16)
    back_low = (back - back_high.astype(np.float64)).astype(np.float32).astype(jnp.bfloat16)
    return high, low, back_high, back_low


def mm(left, right):
    return lax.dot_general(
        left, right, (((1,), (0,)), ((), ())), preferred_element_type=F32
    )


def spectrum(block, high, low):
    return mm(block, high) + mm(block, low)


def invert(spec, back_high, back_low):
    head = spec.astype(BF16)
    tail = (spec - head.astype(F32)).astype(BF16)
    return mm(head, back_high) + (mm(tail, back_high) + mm(head, back_low))


def filter_spectra(filt_ref, high, low, g_ref, channels, blocks, length):
    sign = (1 - 2 * (lax.broadcasted_iota(jnp.int32, (1, length), 1) % 2)).astype(F32)
    before = None
    for lag in range(blocks):
        now = spectrum(filt_ref[:, lag * length : (lag + 1) * length], high, low)
        rows = slice(lag * channels, (lag + 1) * channels)
        if before is None:
            g_ref[rows, :] = now
        else:
            g_ref[rows, :length] = now[:, :length] - sign * before[:, length:]
            g_ref[rows, length:] = now[:, length:] + sign * before[:, :length]
        before = now


def conv_forward_kernel(
    channels, blocks, length, seqs,
    x_ref, filt_ref, high_ref, low_ref, bhigh_ref, blow_ref, out_ref, s_ref, g_ref,
):
    high, low = high_ref[...], low_ref[...]
    filter_spectra(filt_ref, high, low, g_ref, channels, blocks, length)
    for q in range(seqs):
        s_ref[q] = spectrum(x_ref[:, q * length : (q + 1) * length], high, low)

    def tile(step, carry):
        row = pl.multiple_of(step * 8, 8)
        for lane in range(0, length, 128):
            re, im = slice(lane, lane + 128), slice(length + lane, length + lane + 128)
            for q in range(seqs):
                for i in reversed(range(blocks)):
                    acc_re = acc_im = None
                    for j in range(i + 1):
                        s_rows = pl.ds(j * channels + row, 8)
                        g_rows = pl.ds((i - j) * channels + row, 8)
                        sr, si = s_ref[q, s_rows, re], s_ref[q, s_rows, im]
                        gr, gi = g_ref[g_rows, re], g_ref[g_rows, im]
                        new_re = sr * gr - si * gi
                        new_im = sr * gi + si * gr
                        acc_re = new_re if acc_re is None else acc_re + new_re
                        acc_im = new_im if acc_im is None else acc_im + new_im
                    rows = pl.ds(i * channels + row, 8)
                    s_ref[q, rows, re] = acc_re
                    s_ref[q, rows, im] = acc_im
        return carry

    lax.fori_loop(0, channels // 8, tile, 0)
    bhigh, blow = bhigh_ref[...], blow_ref[...]
    for q in range(seqs):
        out_ref[:, q * length : (q + 1) * length] = invert(s_ref[q], bhigh, blow).astype(BF16)


def conv_backward_kernel(
    channels, blocks, length, seqs,
    x_ref, y_ref, filt_ref, high_ref, low_ref, bhigh_ref, blow_ref,
    out_ref, gfilt_ref, s_ref, q_ref, g_ref, l_ref,
):
    high, low = high_ref[...], low_ref[...]
    filter_spectra(filt_ref, high, low, g_ref, channels, blocks, length)
    for q in range(seqs):
        s_ref[q] = spectrum(x_ref[:, q * length : (q + 1) * length], high, low)
        q_ref[q] = spectrum(y_ref[:, q * length : (q + 1) * length], high, low)

    def tile(step, carry):
        row = pl.multiple_of(step * 8, 8)
        for lane in range(0, length, 128):
            re, im = slice(lane, lane + 128), slice(length + lane, length + lane + 128)
            for d in range(blocks):
                acc_re = acc_im = None
                for q in range(seqs):
                    for j in range(blocks - d):
                        s_rows = pl.ds(j * channels + row, 8)
                        y_rows = pl.ds((j + d) * channels + row, 8)
                        sr, si = s_ref[q, s_rows, re], s_ref[q, s_rows, im]
                        yr, yi = q_ref[q, y_rows, re], q_ref[q, y_rows, im]
                        new_re = sr * yr + si * yi
                        new_im = sr * yi - si * yr
                        acc_re = new_re if acc_re is None else acc_re + new_re
                        acc_im = new_im if acc_im is None else acc_im + new_im
                rows = pl.ds(d * channels + row, 8)
                l_ref[rows, re] = acc_re
                l_ref[rows, im] = acc_im
            for q in range(seqs):
                for j in range(blocks):
                    acc_re = acc_im = None
                    for i in range(j, blocks):
                        y_rows = pl.ds(i * channels + row, 8)
                        g_rows = pl.ds((i - j) * channels + row, 8)
                        yr, yi = q_ref[q, y_rows, re], q_ref[q, y_rows, im]
                        gr, gi = g_ref[g_rows, re], g_ref[g_rows, im]
                        new_re = gr * yr + gi * yi
                        new_im = gr * yi - gi * yr
                        acc_re = new_re if acc_re is None else acc_re + new_re
                        acc_im = new_im if acc_im is None else acc_im + new_im
                    rows = pl.ds(j * channels + row, 8)
                    q_ref[q, rows, re] = acc_re
                    q_ref[q, rows, im] = acc_im
        return carry

    lax.fori_loop(0, channels // 8, tile, 0)
    bhigh, blow = bhigh_ref[...], blow_ref[...]
    for q in range(seqs):
        out_ref[:, q * length : (q + 1) * length] = invert(q_ref[q], bhigh, blow).astype(BF16)
    sign = (1 - 2 * (lax.broadcasted_iota(jnp.int32, (1, length), 1) % 2)).astype(F32)
    for d in range(blocks):
        rows = slice(d * channels, (d + 1) * channels)
        real, imag = l_ref[rows, :length], l_ref[rows, length:]
        if d + 1 < blocks:
            after = slice((d + 1) * channels, (d + 2) * channels)
            real = real + sign * l_ref[after, length:]
            imag = imag - sign * l_ref[after, :length]
        both = jnp.concatenate([real, imag], axis=1)
        gfilt_ref[:, d * length : (d + 1) * length] = invert(both, bhigh, blow)


def vmem_spec():
    return pl.BlockSpec(memory_space=pltpu.VMEM)


def conv_forward(x, filt, tables, channels, blocks, length, seqs):
    rows = blocks * channels
    kernel = lambda *refs: conv_forward_kernel(channels, blocks, length, seqs, *refs)
    return pl.pallas_call(
        kernel,
        name="conv_forward",
        out_shape=jax.ShapeDtypeStruct((rows, seqs * length), BF16),
        in_specs=[vmem_spec()] * 6,
        out_specs=vmem_spec(),
        scratch_shapes=[
            pltpu.VMEM((seqs, rows, 2 * length), F32),
            pltpu.VMEM((rows, 2 * length), F32),
        ],
        compiler_params=pltpu.CompilerParams(vmem_limit_bytes=40 << 20),
    )(x, filt, *tables)


def conv_backward(x, y, filt, tables, channels, blocks, length, seqs):
    rows = blocks * channels
    kernel = lambda *refs: conv_backward_kernel(channels, blocks, length, seqs, *refs)
    return pl.pallas_call(
        kernel,
        name="conv_backward",
        out_shape=(
            jax.ShapeDtypeStruct((rows, seqs * length), BF16),
            jax.ShapeDtypeStruct((channels, blocks * length), F32),
        ),
        in_specs=[vmem_spec()] * 7,
        out_specs=(vmem_spec(), vmem_spec()),
        scratch_shapes=[
            pltpu.VMEM((seqs, rows, 2 * length), F32),
            pltpu.VMEM((seqs, rows, 2 * length), F32),
            pltpu.VMEM((rows, 2 * length), F32),
            pltpu.VMEM((rows, 2 * length), F32),
        ],
        compiler_params=pltpu.CompilerParams(vmem_limit_bytes=48 << 20),
    )(x, y, filt, *tables)


def shifted(block, axis, distance):
    count = lax.axis_size(axis)
    route = [(i - distance, i) for i in range(count) if 0 <= i - distance < count]
    return lax.ppermute(block, axis, route)


def local(
    tokens, cotangent, lengths, decay_rate, norm1_gain, norm1_bias, w_in, b_in,
    short_weight, short_bias, filter_w1, filter_b1, filter_w2, filter_b2, filter_w3,
    skip_gain, w_out, b_out, norm2_gain, norm2_bias, mlp_w1, mlp_b1, mlp_w2, mlp_b2,
):
    seqs, block, width = tokens.shape[1:]
    rows = seqs * block
    blocks = lax.axis_size("seq")
    full = blocks * block
    channels = width // blocks
    position = lax.axis_index("seq")
    tables = [jnp.asarray(t) for t in transform_tables(block)]

    def col(vector):
        return vector.astype(F32)[:, None]

    edge_tokens = shifted(tokens[0, :, block - 2 :, :], "seq", 1).reshape(2 * seqs, width)
    inputs = tokens.reshape(rows, width).astype(F32)
    gain_one = norm1_gain.astype(F32)
    bias_one = norm1_bias.astype(F32)
    normed, unit_one, inverse_one = norm_forward(inputs, gain_one, bias_one)
    normed_low = normed.astype(BF16)
    edge_normed = norm_forward(edge_tokens.astype(F32), gain_one, bias_one)[0].astype(BF16)

    mixed = (dot(w_in, normed_low, ((0,), (1,))) + col(b_in)).astype(BF16)
    mixed = mixed.reshape(3 * width, seqs, block)
    edge = (dot(w_in, edge_normed, ((0,), (1,))) + col(b_in)).astype(BF16)
    edge = jnp.where(position > 0, edge, jnp.zeros_like(edge)).reshape(3 * width, seqs, 2)
    extended = jnp.concatenate([edge, mixed], axis=2).astype(F32)
    taps = short_weight.astype(F32)[:, :, None, None]
    conv = (
        taps[0] * extended[:, :, 2:]
        + taps[1] * extended[:, :, 1:-1]
        + taps[2] * extended[:, :, :-2]
        + short_bias.astype(F32)[:, None, None]
    ).reshape(3 * width, rows)
    gate_out = conv[:width]
    gate_in = conv[width : 2 * width]
    values = conv[2 * width :]
    signal_low = (values * gate_in).astype(BF16)
    signal = signal_low.astype(F32)
    skip = col(skip_gain)
    signal_all = lax.all_to_all(signal_low, "seq", 0, 0, tiled=True)

    own = position * channels
    rates = lax.dynamic_slice_in_dim(decay_rate, own, channels)
    weight_three = lax.dynamic_slice_in_dim(filter_w3.astype(F32), own, channels, axis=1)

    def filter_fn(weight_one, bias_first, weight_two, bias_second, weight_last):
        return filter_values(
            weight_one, bias_first, weight_two, bias_second, weight_last, rates, full
        )

    raw_filter, filter_pull = jax.vjp(
        filter_fn,
        filter_w1.astype(F32),
        filter_b1.astype(F32),
        filter_w2.astype(F32),
        filter_b2.astype(F32),
        weight_three,
    )
    filt = raw_filter.astype(BF16)
    long_all = conv_forward(signal_all, filt, tables, channels, blocks, block, seqs)
    conv_long = lax.all_to_all(long_all, "seq", 0, 0, tiled=True).astype(F32)
    long_out = conv_long + signal * skip
    gated_low = (long_out * gate_out).astype(BF16)

    branch = dot(gated_low, w_out, ((0,), (0,))) + b_out.astype(F32)
    resid = inputs + branch
    gain_two = norm2_gain.astype(F32)
    normed_two, unit_two, inverse_two = norm_forward(resid, gain_two, norm2_bias.astype(F32))
    normed_two_low = normed_two.astype(BF16)
    pre = dot(normed_two_low, mlp_w1, ((1,), (0,))) + mlp_b1.astype(F32)
    cumulative = 0.5 * (1.0 + lax.erf(pre * (1.0 / math.sqrt(2.0))))
    density = jnp.exp(-0.5 * pre * pre) * (1.0 / math.sqrt(2.0 * math.pi))
    active_low = (pre * cumulative).astype(BF16)
    final = resid + dot(active_low, mlp_w2, ((1,), (0,))) + mlp_b2.astype(F32)
    places = position * block + jnp.arange(block, dtype=jnp.int32)
    valid = (places[None, :] < lengths[0][:, None]).astype(F32).reshape(rows, 1)
    output = (final * valid).astype(BF16).reshape(1, seqs, block, width)
    grad_final_low = (cotangent.reshape(rows, width).astype(F32) * valid).astype(BF16)
    grad_final = grad_final_low.astype(F32)
    grad_mlp_b2 = jnp.sum(grad_final, axis=0)
    grad_mlp_w2 = dot(active_low, grad_final_low, ((0,), (0,)))
    grad_active = dot(grad_final_low, mlp_w2, ((1,), (1,)))
    grad_pre_low = (grad_active * (cumulative + pre * density)).astype(BF16)
    grad_mlp_b1 = jnp.sum(grad_pre_low.astype(F32), axis=0)
    grad_mlp_w1 = dot(normed_two_low, grad_pre_low, ((0,), (0,)))
    grad_normed_two = dot(grad_pre_low, mlp_w1, ((1,), (1,)))
    grad_resid_norm, grad_norm2_gain, grad_norm2_bias = norm_backward(
        grad_normed_two, gain_two, unit_two, inverse_two
    )
    grad_resid = grad_final + grad_resid_norm
    grad_branch_low = grad_resid.astype(BF16)
    grad_b_out = jnp.sum(grad_branch_low.astype(F32), axis=0)
    grad_w_out = dot(gated_low, grad_branch_low, ((1,), (0,)))

    grad_gated = dot(w_out, grad_branch_low, ((1,), (1,)))
    grad_long_low = (grad_gated * gate_out).astype(BF16)
    grad_long = grad_long_low.astype(F32)
    grad_gate_out = grad_gated * long_out
    grad_skip_gain = jnp.sum(grad_long * signal, axis=1)
    grad_long_all = lax.all_to_all(grad_long_low, "seq", 0, 0, tiled=True)
    back_all, grad_filter = conv_backward(
        signal_all, grad_long_all, filt, tables, channels, blocks, block, seqs
    )
    grad_signal = lax.all_to_all(back_all, "seq", 0, 0, tiled=True).astype(F32)
    grad_signal = grad_signal + grad_long * skip
    grad_filter_w1, grad_filter_b1, grad_filter_w2, grad_filter_b2, own_w3 = filter_pull(
        grad_filter
    )
    grad_filter_w3 = lax.dynamic_update_slice_in_dim(
        jnp.zeros(filter_w3.shape, F32), own_w3, own, axis=1
    )
    grad_conv = jnp.concatenate(
        [grad_gate_out, grad_signal * values, grad_signal * gate_in], axis=0
    )
    grad_short_bias = jnp.sum(grad_conv, axis=1)
    grad_conv = grad_conv.reshape(3 * width, seqs, block)
    grad_short_weight = jnp.stack(
        [
            jnp.sum(grad_conv * extended[:, :, 2:], axis=(1, 2)),
            jnp.sum(grad_conv * extended[:, :, 1:-1], axis=(1, 2)),
            jnp.sum(grad_conv * extended[:, :, :-2], axis=(1, 2)),
        ]
    )
    after = shifted(grad_conv[:, :, :2].reshape(3 * width, 2 * seqs), "seq", -1)
    after = after.reshape(3 * width, seqs, 2)
    grown = jnp.concatenate([grad_conv, after], axis=2)
    grad_mixed = (
        taps[0] * grown[:, :, :-2] + taps[1] * grown[:, :, 1:-1] + taps[2] * grown[:, :, 2:]
    )
    grad_mixed_low = grad_mixed.astype(BF16).reshape(3 * width, rows)
    grad_b_in = jnp.sum(grad_mixed_low.astype(F32), axis=1)
    grad_w_in = dot(normed_low, grad_mixed_low, ((0,), (1,)))
    grad_normed = dot(grad_mixed_low, w_in, ((0,), (1,)))
    grad_input_norm, grad_norm1_gain, grad_norm1_bias = norm_backward(
        grad_normed, gain_one, unit_one, inverse_one
    )
    tokens_grad = (grad_resid + grad_input_norm).reshape(1, seqs, block, width)

    small = [
        grad_norm1_gain, grad_norm1_bias, grad_b_in, grad_short_weight, grad_short_bias,
        grad_filter_w1, grad_filter_b1, grad_filter_w2, grad_filter_b2, grad_filter_w3,
        grad_skip_gain, grad_b_out, grad_norm2_gain, grad_norm2_bias, grad_mlp_b1,
        grad_mlp_b2,
    ]
    flat = jnp.concatenate([part.reshape(-1) for part in small])
    padding = -flat.shape[0] % width
    flat = jnp.pad(flat, (0, padding)).reshape(-1, width)
    sums = lax.psum(
        tuple(
            part.astype(BF16)
            for part in (grad_w_in, grad_w_out, grad_mlp_w1, grad_mlp_w2, flat)
        ),
        ("bucket", "seq"),
    )
    sum_w_in, sum_w_out, sum_w1, sum_w2, sum_flat = (part.astype(F32) for part in sums)
    sum_flat = sum_flat.reshape(-1)
    pieces = []
    start = 0
    for part in small:
        pieces.append(sum_flat[start : start + part.size].reshape(part.shape))
        start += part.size
    return (
        output, tokens_grad, pieces[0], pieces[1], sum_w_in, pieces[2], pieces[3], pieces[4],
        pieces[5], pieces[6], pieces[7], pieces[8], pieces[9], pieces[10], sum_w_out,
        pieces[11], pieces[12], pieces[13], sum_w1, pieces[14], sum_w2, pieces[15],
    )


def solution(mesh):
    split = P("bucket", None, "seq", None)
    in_specs = (split, split, P("bucket", None)) + (P(),) * 21
    out_specs = (split, split) + (P(),) * 20
    return jax.shard_map(local, mesh=mesh, in_specs=in_specs, out_specs=out_specs, check_vma=False)
```

time: 1690 us -> 596 us (0.35)
  waiting for transfers between devices: 1180 us -> 268 us
  other arithmetic: 224 us -> 81.2 us
  matrix products: 160 us -> 79.1 us
  starting transfers between devices: 6.73 us -> 25.2 us
  Pallas kernels: 0 us -> 17.8 us
    all_gather x4 -> x0, waiting for transfers between devices: 609 us -> none  [the longest x1 177 us: local(): lax.all_gather(sig_imag[None], 'seq', axis=0, tiled=True)]
    psum x2 -> x1, waiting for transfers between devices: 567 us -> 246 us  [local(): lax.psum(tuple((part.astype(BF16) for part in (grad_w_in, grad_w_out, gra...]
    dot_general x36 -> x21, matrix products: 160 us -> 79.1 us  [the longest x13 57.4 us: dot(): lax.dot_general(left, right, (dims, ((), ())), preferred_element_type=F32)]
    add x13 -> x4, other arithmetic: 59.1 us -> 3.78 us  [the longest x1 1.69 us: local(): tokens_grad = (grad_resid + grad_input_norm).reshape(1, seqs, block, width)]
    reduce_sum x12 -> x4, other arithmetic: 65.1 us -> 16.6 us  [the longest x1 7.19 us: local(): jnp.sum(grad_conv * extended[:, :, 2:], axis=(1, 2))]
    mul x19 -> x2, other arithmetic: 48.5 us -> 3.06 us  [the longest x1 3.06 us: local(): grad_signal * values]
    unnamed x289 -> x195, local copies, waits for them, and re-layouts: 53.7 us -> 17.7 us
    convert_element_type x37 -> x26, other arithmetic: 17.5 us -> 43.4 us  [the longest x5 18.3 us: local(): part.astype(F32)]
  transfers between devices with their start and end apart: 8 -> 7, of which waited for: 6 -> 5; matrix products, arithmetic and copies ran while one was open for 9% -> 14% of each run, Pallas kernels for 0% -> 0%
where the time goes in v1:
time: 596 us; the launch traced here: 587 us
  waiting for transfers between devices  268 us (45%)
  local copies, waits for them, and re-layouts  100 us (17%)
  other arithmetic  81.2 us (14%)
  matrix products  79.1 us (13%)
  starting transfers between devices  25.2 us (4%)
  Pallas kernels  17.8 us (3%)
  between operations  15.3 us (3%)
    psum x1, waiting for transfers between devices, local(): lax.psum(tuple((part.astype(BF16) for part in (grad_w_in, grad_w_out, gra...  246 us
    dot_general x13, matrix products, dot(): lax.dot_general(left, right, (dims, ((), ())), preferred_element_type=F32)  57.4 us
    concatenate x1, local copies, waits for them, and re-layouts, local(): flat = jnp.concatenate([part.reshape(-1) for part in small])  21.7 us
    dot_general x8, matrix products, precise(): jnp.einsum(formula, left, right, precision=HIGH, preferred_element_type=F32)  21.7 us
    convert_element_type x5, other arithmetic, local(): part.astype(F32)  18.3 us
    unnamed x195, local copies, waits for them, and re-layouts  17.7 us
    slice x12, local copies, waits for them, and re-layouts, local(): pieces.append(sum_flat[start:start + part.size].reshape(part.shape))  16.6 us
  transfers between devices with their start and end apart: 7, of which 5 were waited for; matrix products, arithmetic and copies ran while one was open for 14% of the time, Pallas kernels for 0%

profile of v1, /device:TPU:0, one launch (start us, length us, event | category | flops | bytes accessed | tf_op | source)
XLA Modules:
  0.0 586.7 jit_solution(181624771214016175)
XLA Ops:
  8.8 5.4 collective-permute-start
  19.4 3.4 fusion.12
  44.2 3.1 convert_element_type.271
  47.3 4.6 all-to-all-start
  56.2 3.7 fusion.82
  66.7 5.4 all-to-all-done
  76.9 7.0 %conv_forward.1 = bf16[768,512]{1,0:T(8,128)(2,1)S(1)} custom-call(bf16[768,512]{1,0:T(8,128)(2,1)} %bitcast.5.refs_0_, bf16[96,2048]{1,0:T(8,128)(2,1)S(1)} %copy-done.1, bf16[256,512]{1,0:T(8,128)(2,1)S(1)} %copy-done.12, bf16[256,512]{1,0:T(8,128)(2,1)S(1)} %copy-done.10, bf16[512,256]{1,0:T(8,128)(2,1)S(1)} %copy-done.8, bf16[512,256]{1,0:T(8,128)(2,1)S(1)} %copy-done.6), custom_call_target="tpu_custom_call" | custom-call | tf_op jit(solution)/shard_map/conv_forward/pallas_call | solution.py:208
  84.8 4.7 all-to-all-start.1
  100.2 9.1 %all-to-all-done.1 = bf16[8,96,512]{2,1,0:T(8,128)(2,1)} async-done(((bf16[8,96,512]{2,1,0:T(8,128)(2,1)}), bf16[8,96,512]{2,1,0:T(8,128)(2,1)}, u32[]{:S(2)}, u32[]{:S(2)}) %all-to-all-start.1) | async-done | bytes 786464 | tf_op jit(solution)/shard_map/all_to_all | solution.py:313
  114.8 3.4 fusion.22
  120.0 7.0 %multiply_convert_fusion = (bf16[512,3072]{1,0:T(8,128)(2,1)}, f32[512,3072]{1,0:T(8,128)S(1)}) fusion(f32[3072]{0:T(1024)S(1)} %copy-done.71, bf16[768,3072]{1,0:T(8,128)(2,1)} %param.48, f32[512,768]{1,0:T(8,128)S(1)} %get-tuple-element.86, f32[768]{0:T(1024)S(1)} %copy-done.78, f32[768]{0:T(1024)S(1)} %copy-done.69, f32[512]{0:T(512)S(1)} %add_rsqrt_fusion, ...), kind=kOutput, calls=%fused_computation.7 | convolution fusion | flops 2427322368 | bytes 15751168 | tf_op jit(solution)/shard_map/dot_general | solution.py:39
  127.0 5.2 fusion.87
  132.3 3.5 multiply_reduce_fusion.3
  143.0 4.4 all-to-all-start.2
  150.0 6.9 %convolution_convert_fusion = bf16[3072,768]{1,0:T(8,128)(2,1)} fusion(bf16[512,3072]{1,0:T(8,128)(2,1)} %get-tuple-element.87, bf16[512,768]{1,0:T(8,128)(2,1)S(1)} %copy-done.45), kind=kOutput, calls=%fused_computation.9 | convolution fusion | flops 2418278400 | bytes 8650752 | tf_op jit(solution)/shard_map/dot_general | solution.py:39
  156.9 4.8 convolution_convert_fusion.1
  161.7 5.5 all-to-all-done.2
  172.0 10.8 %conv_backward.1 = (bf16[768,512]{1,0:T(8,128)(2,1)S(1)}, f32[96,2048]{1,0:T(8,128)S(1)}) custom-call(bf16[768,512]{1,0:T(8,128)(2,1)} %bitcast.5.refs_0_, bf16[768,512]{1,0:T(8,128)(2,1)} %bitcast.16.refs_1_, bf16[96,2048]{1,0:T(8,128)(2,1)S(1)} %copy-done.2, bf16[256,512]{1,0:T(8,128)(2,1)S(1)} %copy-done.13, bf16[256,512]{1,0:T(8,128)(2,1)S(1)} %copy-done.11, ...), custom_call_target="tpu_custom_call" | custom-call | tf_op jit(solution)/shard_map/conv_backward/pallas_call | solution.py:225
  184.6 4.2 all-to-all-start.3
  189.1 3.6 convolution_convert_fusion.3
  192.7 3.7 fusion.86
  206.4 3.9 fusion.85
  221.5 7.2 %multiply_reduce_fusion.2 = (bf16[2304]{0:T(1024)(128)(2,1)S(1)}, bf16[2304]{0:T(1024)(128)(2,1)S(1)}, bf16[2304]{0:T(1024)(128)(2,1)S(1)}) fusion(f32[2304,2,258]{0,2,1:T(8,128)} %copy-done.15, f32[768,512]{0,1:T(8,128)S(1)} %get-tuple-element.62, f32[768,512]{0,1:T(8,128)S(1)} %get-tuple-element.61, f32[768,512]{0,1:T(8,128)S(1)} %copy-done.24), kind=kLoop, calls=%fused_computation.25 | loop fusion | flops 9430272 | bytes 18888192 | tf_op jit(solution)/shard_map/reduce_sum | solution.py:371
  241.7 7.1 %fusion.75 = (bf16[2304]{0:T(1024)(128)(2,1)}, bf16[2304,2,256]{0,2,1:T(8,128)(2,1)S(1)}) fusion(f32[2304,2,2]{0,2,1:T(2,128)} %reshape.343, f32[2304,2,256]{0,2,1:T(8,128)} %bitcast.133, f32[2304]{0:T(1024)} %get-tuple-element.40, f32[2304]{0:T(1024)} %get-tuple-element.41, f32[2304]{0:T(1024)S(1)} %copy-done.47), kind=kLoop, calls=%fused_computation.155 | loop fusion | flops 10614528 | bytes 7147008 | tf_op jit(solution)/shard_map/reduce_sum | solution.py:383
  248.8 4.0 fusion.41
  252.8 21.7 %concatenate.20 = bf16[75456]{0:T(1024)(128)(2,1)} concatenate(bf16[768]{0:T(1024)(128)(2,1)} %get-tuple-element.31, bf16[768]{0:T(1024)(128)(2,1)} %get-tuple-element.36, bf16[2304]{0:T(1024)(128)(2,1)} %get-tuple-element.51, bf16[6912]{0:T(1024)(128)(2,1)} %reshape.346, bf16[2304]{0:T(1024)(128)(2,1)} %get-tuple-element.55, bf16[2112]{0:T(1024)(128)(2,1)} %reshape.347, ...), dimensions={0} | concatenate | bytes 301824 | tf_op jit(solution)/shard_map/concatenate | solution.py:397
  277.8 5.7 convolution_convert_fusion.2
  284.3 7.4 %multiply_convert_fusion.2 = bf16[512,768]{1,0:T(8,128)(2,1)} fusion(f32[512,768]{1,0:T(8,128)} %copy-done.27, bf16[512,3072]{1,0:T(8,128)(2,1)} %get-tuple-element.87, bf16[3072,768]{1,0:T(8,128)(2,1)} %param.50, f32[512]{0:T(512)S(1)} %bitcast.150, f32[768]{0:T(1024)S(1)} %convert_element_type.290), kind=kOutput, calls=%fused_computation.82 | convolution fusion | flops 2417491968 | bytes 10228736 | tf_op jit(solution)/shard_map/dot_general | solution.py:39
  293.4 245.9 %all-reduce.4.cloned.1.call-done = (bf16[99,768]{1,0:T(8,128)(2,1)}, bf16[768,2304]{1,0:T(8,128)(2,1)}, bf16[768,768]{1,0:T(8,128)(2,1)}, bf16[768,3072]{1,0:T(8,128)(2,1)}, bf16[3072,768]{1,0:T(8,128)(2,1)}) async-done(((bf16[99,768]{1,0:T(8,128)(2,1)}, bf16[768,2304]{1,0:T(8,128)(2,1)}, bf16[768,768]{1,0:T(8,128)(2,1)}, bf16[768,3072]{1,0:T(8,128)(2,1)}, bf16[3072,768]{1,0:T(8,128)(2,1)}), ...) | async-done | bytes 14307856 | tf_op jit(solution)/shard_map/psum | solution.py:400
  565.3 4.1 convert_element_type.317
  569.9 5.0 convert_element_type.321
  574.9 4.5 convert_element_type.323
  (302 shorter events, 145.4 us)
Async XLA Ops:
  7.2 12.2 %copy-start = (bf16[768,2304]{1,0:T(8,128)(2,1)S(1)}, bf16[768,2304]{1,0:T(8,128)(2,1)}, u32[]{:S(2)}) copy-start(bf16[768,2304]{1,0:T(8,128)(2,1)} %param.34) | copy-start | bytes 10616836
  7.2 11.8 %copy-start.18 = (bf16[1,2,256,768]{3,2,1,0:T(8,128)(2,1)S(1)}, bf16[1,2,256,768]{3,2,1,0:T(8,128)(2,1)}, u32[]{:S(2)}) copy-start(bf16[1,2,256,768]{3,2,1,0:T(8,128)(2,1)} %param.28) | copy-start | bytes 2359300
  7.2 11.0 %copy-start.81 = (bf16[768]{0:T(1024)(128)(2,1)S(1)}, bf16[768]{0:T(1024)(128)(2,1)}, u32[]{:S(2)}) copy-start(bf16[768]{0:T(1024)(128)(2,1)} %param.32) | copy-start | bytes 4612
  7.2 11.0 %copy-start.82 = (bf16[768]{0:T(1024)(128)(2,1)S(1)}, bf16[768]{0:T(1024)(128)(2,1)}, u32[]{:S(2)}) copy-start(bf16[768]{0:T(1024)(128)(2,1)} %param.33) | copy-start | bytes 4612
  7.2 11.0 %copy-start.75 = (bf16[2304]{0:T(1024)(128)(2,1)S(1)}, bf16[2304]{0:T(1024)(128)(2,1)}, u32[]{:S(2)}) copy-start(bf16[2304]{0:T(1024)(128)(2,1)} %param.35) | copy-start | bytes 13828
  7.2 11.0 %copy-start.68 = (bf16[3,2304]{1,0:T(4,128)(2,1)S(1)}, bf16[3,2304]{1,0:T(4,128)(2,1)}, u32[]{:S(2)}) copy-start(bf16[3,2304]{1,0:T(4,128)(2,1)} %param.36) | copy-start | bytes 41476
  8.8 15.3 %collective-permute-start = (bf16[2,2,768]{2,1,0:T(2,128)(2,1)}, bf16[2,2,768]{2,1,0:T(2,128)(2,1)}, u32[]{:S(2)}, u32[]{:S(2)}) collective-permute-start(bf16[2,2,768]{2,1,0:T(2,128)(2,1)} %slice_bitcast_fusion), channel_id=1, source_target_pairs={{0,1},{1,2},{2,3},{3,4},{4,5},{5,6},{6,7},{8,9},{9,10},{10,11},{11... | collective-permute-start | bytes 18440 | tf_op jit(solution)/shard_map/ppermute | solution.py:247
  18.3 12.5 %copy-start.52 = (f32[768]{0:T(1024)}, f32[768]{0:T(1024)S(1)}, u32[]{:S(2)}) copy-start(f32[768]{0:T(1024)S(1)} %convert_element_type.260) | copy-start | bytes 9220
  44.2 8.3 %copy-start.87 = (bf16[64]{0:T(256)(128)(2,1)S(1)}, bf16[64]{0:T(256)(128)(2,1)}, u32[]{:S(2)}) copy-start(bf16[64]{0:T(256)(128)(2,1)} %param.39) | copy-start | bytes 388
  47.3 24.7 %all-to-all-start = ((bf16[8,96,512]{2,1,0:T(8,128)(2,1)}), bf16[8,96,512]{2,1,0:T(8,128)(2,1)}, u32[]{:S(2)}, u32[]{:S(2)}) async-start(bf16[8,96,512]{2,1,0:T(8,128)(2,1)} %convert_element_type.271), calls=%async_computation | async-start | bytes 1572864 | tf_op jit(solution)/shard_map/all_to_all | solution.py:292
  55.0 8.7 %copy-start.76 = (f32[96]{0:T(128)}, f32[96]{0:T(128)S(1)}, u32[]{:S(2)}) copy-start(f32[96]{0:T(128)S(1)} %dynamic_slice.7) | copy-start | bytes 1156
  84.8 24.5 %all-to-all-start.1 = ((bf16[8,96,512]{2,1,0:T(8,128)(2,1)}), bf16[8,96,512]{2,1,0:T(8,128)(2,1)}, u32[]{:S(2)}, u32[]{:S(2)}) async-start(bf16[8,96,512]{2,1,0:T(8,128)(2,1)} %bitcast.130), calls=%async_computation.1 | async-start | bytes 1572864 | tf_op jit(solution)/shard_map/all_to_all | solution.py:313
  90.3 7.7 %copy-start.63 = (f32[1,2,2,128]{3,1,2,0:T(2,128)}, f32[1,2,2,128]{3,1,2,0:T(2,128)S(1)}, u32[]{:S(2)}) copy-start(f32[1,2,2,128]{3,1,2,0:T(2,128)S(1)} %copy.60) | copy-start | bytes 6148
  119.1 16.7 %copy-start.27 = (f32[512,768]{1,0:T(8,128)}, f32[512,768]{1,0:T(8,128)S(1)}, u32[]{:S(2)}) copy-start(f32[512,768]{1,0:T(8,128)S(1)} %get-tuple-element.86) | copy-start | bytes 4718596
  119.2 16.6 %copy-start.66 = (f32[512]{0:T(512)}, f32[512]{0:T(512)S(1)}, u32[]{:S(2)}) copy-start(f32[512]{0:T(512)S(1)} %broadcast_multiply_fusion.4) | copy-start | bytes 6148
  119.2 7.8 %slice-start.4 = ((s8[4718592]{0:T(1024)(128)(4,1)}), s8[4194304]{0:T(1024)(128)(4,1)S(1)}, s32[]{:S(2)}) async-start(s8[4718592]{0:T(1024)(128)(4,1)} %bitcast.154), calls=%async_computation.9 | async-start | bytes 8388608
  120.0 15.9 %copy-start.73 = (f32[512]{0:T(512)}, f32[512]{0:T(512)S(1)}, u32[]{:S(2)}) copy-start(f32[512]{0:T(512)S(1)} %add_rsqrt_fusion) | copy-start | bytes 6148
  120.0 12.3 %slice-start.2 = ((s8[4718592]{0:T(1024)(128)(4,1)}), s8[4194304]{0:T(1024)(128)(4,1)S(1)}, s32[]{:S(2)}) async-start(s8[4718592]{0:T(1024)(128)(4,1)} %bitcast.152), calls=%async_computation.7 | async-start | bytes 8388608
  143.0 24.2 %all-to-all-start.2 = ((bf16[8,96,512]{2,1,0:T(8,128)(2,1)}), bf16[8,96,512]{2,1,0:T(8,128)(2,1)}, u32[]{:S(2)}, u32[]{:S(2)}) async-start(bf16[8,96,512]{2,1,0:T(8,128)(2,1)} %bitcast.136), calls=%async_computation.2 | async-start | bytes 1572864 | tf_op jit(solution)/shard_map/all_to_all | solution.py:352
  184.6 28.3 %all-to-all-start.3 = ((bf16[8,96,512]{2,1,0:T(8,128)(2,1)}), bf16[8,96,512]{2,1,0:T(8,128)(2,1)}, u32[]{:S(2)}, u32[]{:S(2)}) async-start(bf16[8,96,512]{2,1,0:T(8,128)(2,1)} %bitcast.131), calls=%async_computation.3 | async-start | bytes 1572864 | tf_op jit(solution)/shard_map/all_to_all | solution.py:356
  188.8 350.4 %all-reduce.4.cloned.1.call-start = ((), (), s32[]{:S(2)}) async-start(), calls=%async_computation.4 | async-start | bytes 28631040 | tf_op jit(solution)/shard_map/psum | solution.py:400
  202.7 7.6 %copy-start.50 = (f32[1,2048]{1,0:T(1,128)S(1)}, f32[1,2048]{1,0:T(1,128)}, u32[]{:S(2)}) copy-start(f32[1,2048]{1,0:T(1,128)} %convert_multiply_fusion.4) | copy-start | bytes 24580
  228.7 13.0 %copy-start.47 = (f32[2304]{0:T(1024)S(1)}, f32[2304]{0:T(1024)}, u32[]{:S(2)}) copy-start(f32[2304]{0:T(1024)} %get-tuple-element.39) | copy-start | bytes 27652
  234.1 6.2 %collective-permute-start.1 = (f32[2304,4]{0,1:T(4,128)}, f32[2304,4]{0,1:T(4,128)}, u32[]{:S(2)}, u32[]{:S(2)}) collective-permute-start(f32[2304,4]{0,1:T(4,128)} %reshape.342), channel_id=1, source_target_pairs={{1,0},{2,1},{3,2},{4,3},{5,4},{6,5},{7,6},{9,8},{10,9},{11,10},{12... | collective-permute-start | bytes 110600 | tf_op jit(solution)/shard_map/ppermute | solution.py:247
  284.2 7.4 %copy-start.85 = (f32[512]{0:T(512)S(1)}, f32[512]{0:T(512)}, u32[]{:S(2)}) copy-start(f32[512]{0:T(512)} %get-tuple-element.32) | copy-start | bytes 6148
  284.2 7.4 %copy-start.84 = (f32[512]{0:T(512)S(1)}, f32[512]{0:T(512)}, u32[]{:S(2)}) copy-start(f32[512]{0:T(512)} %get-tuple-element.33) | copy-start | bytes 6148
  284.2 7.4 %copy-start.17 = (f32[512,768]{1,0:T(8,128)S(1)}, f32[512,768]{1,0:T(8,128)}, u32[]{:S(2)}) copy-start(f32[512,768]{1,0:T(8,128)} %copy-done.16) | copy-start | bytes 4718596
  284.2 7.4 %copy-start.21 = (bf16[1,2,256,768]{3,2,1,0:T(8,128)(2,1)S(1)}, bf16[1,2,256,768]{3,2,1,0:T(8,128)(2,1)}, u32[]{:S(2)}) copy-start(bf16[1,2,256,768]{3,2,1,0:T(8,128)(2,1)} %param.28) | copy-start | bytes 2359300
  284.2 7.4 %copy-start.38 = (f32[512,768]{1,0:T(8,128)S(1)}, f32[512,768]{1,0:T(8,128)}, u32[]{:S(2)}) copy-start(f32[512,768]{1,0:T(8,128)} %get-tuple-element.90) | copy-start | bytes 4718596
  284.3 7.4 %copy-start.59 = (f32[1,2,2,128]{3,1,2,0:T(2,128)S(1)}, f32[1,2,2,128]{3,1,2,0:T(2,128)}, u32[]{:S(2)}) copy-start(f32[1,2,2,128]{3,1,2,0:T(2,128)} %copy-done.57) | copy-start | bytes 6148
  284.3 7.4 %copy-start.62 = (f32[1,2,2,128]{3,1,2,0:T(2,128)S(1)}, f32[1,2,2,128]{3,1,2,0:T(2,128)}, u32[]{:S(2)}) copy-start(f32[1,2,2,128]{3,1,2,0:T(2,128)} %copy-done.60) | copy-start | bytes 6148
  565.3 9.6 %slice-start = ((s8[4718592]{0:T(1024)(128)(4,1)}), s8[4194304]{0:T(1024)(128)(4,1)S(1)}, s32[]{:S(2)}) async-start(s8[4718592]{0:T(1024)(128)(4,1)} %bitcast.134), calls=%async_computation.5 | async-start | bytes 8388608
  (71 other events, 227.7 us)
Sparse Core Ops, SparseCore 0:
  283.7 255.5 all-reduce.3
